TPU v7x, 512 devices: a whole 4x4x16 slice. The times are simulated.
512 devices in a mesh: row: 16 (over y, x_hi, core), col: 32 (over x_lo, z).
Axes of the slice: x: 4 (x_hi: 2, x_lo: 2; x = x_hi * 2 + x_lo), y: 4, z: 16, core: 2. Of those that a mesh axis runs over, the one named last changes fastest.
Arguments:
- vectors: bfloat16 [393216, 1024], P(('row', 'col')), may hold values from -6 to 6
- ham_blocks: bfloat16 [3072, 5, 128, 128], P(('row', 'col')), as said below
- ham_columns: int32 [3072, 5], P(('row', 'col')), may hold values from 0 to 3071, as said below
- bounds: float32 [2], replicated, may hold values from -1 to 2.6, as said below
Outputs:
- filtered: bfloat16 [393216, 1024], P(('row', 'col'))
Inputs may be any that keep to these rules, and one draw needn't show every extreme that they name: `ham_columns`: each slot of block row g names a block column (g + o) mod 3072 with -2 <= o <= 2; some slot names g itself, every other distance at most once. Slots whose offset is absent name g itself and carry zero blocks; the one slot with offset 0 carries the diagonal block. `ham_blocks`: H is symmetric: the block of block row g at block column h is the transpose of the block of block row h at block column g. bounds[0] < bounds[1].
All inputs are finite; a program needn't handle non-finite values.
Results may differ from a plain program's by a relative error of at most 0.0045.
Values may be sent and summed in bfloat16 or wider, within the bound.
A program may use at most 64 MiB of HBM per device.

v0:
```python
import jax
import jax.numpy as jnp
from jax import lax
from jax.sharding import PartitionSpec as P

REACH = 2
DEG = 2


def extended(cells, sides, width):
    for axis, dim in sides:
        count = lax.axis_size(axis)
        head = lax.slice_in_dim(cells, 0, width, axis=dim)
        tail = lax.slice_in_dim(cells, cells.shape[dim] - width, cells.shape[dim], axis=dim)
        cells = jnp.concatenate(
            [
                lax.ppermute(tail, axis, [(i, (i + 1) % count) for i in range(count)]),
                cells,
                lax.ppermute(head, axis, [((i + 1) % count, i) for i in range(count)]),
            ],
            axis=dim,
        )
    return cells


def per_device(vectors, ham_blocks, ham_columns, bounds):
    rows_here = ham_blocks.shape[0]
    block_size = ham_blocks.shape[2]
    vec_width = vectors.shape[1]
    total_blocks = lax.axis_size(("row", "col")) * rows_here
    first = lax.axis_index(("row", "col")) * rows_here
    center = 0.5 * (bounds[1] + bounds[0])
    halfwidth = 0.5 * (bounds[1] - bounds[0])
    previous = vectors
    current = vectors
    for degree_step in range(DEG):
        padded = extended(current, ((("row", "col"), 0),), REACH * block_size)
        local_index = jnp.remainder(ham_columns - first + REACH, total_blocks)
        grid = padded.reshape(-1, block_size, vec_width)
        picked = jnp.take(grid, local_index, axis=0)
        product = jnp.einsum(
            "rkij,rkjm->rim", ham_blocks, picked, preferred_element_type=jnp.float32
        )
        image = product.reshape(ham_blocks.shape[0] * block_size, vec_width)
        shifted = (image - center * current.astype(jnp.float32)) / halfwidth
        if degree_step == 0:
            updated = shifted
        else:
            updated = 2.0 * shifted - previous.astype(jnp.float32)
        previous, current = (current, updated.astype(jnp.bfloat16))
    return current


def solution(mesh):
    return jax.shard_map(
        per_device,
        mesh=mesh,
        in_specs=(
            P(("row", "col"), None),
            P(("row", "col"), None, None, None),
            P(("row", "col"), None),
            P(),
        ),
        out_specs=P(("row", "col"), None),
        check_vma=False,
    )
```

profile of v0, /device:TPU:24, one launch (start us, length us, event | category | flops | bytes accessed | tf_op | source)
XLA Modules:
  0.0 79.2 jit_solution(13876533929321705302)
XLA Ops:
  0.0 0.0 copy-start
  0.0 2.4 %fusion.17 = (bf16[256,1024]{1,0:T(8,128)(2,1)}, bf16[256,1024]{1,0:T(8,128)(2,1)}) fusion(bf16[768,1024]{1,0:T(8,128)(2,1)} %param.6), kind=kLoop, calls=%fused_computation.29 | loop fusion | bytes 2097152 | tf_op jit(solution)/shard_map/slice | solution.py:14
  2.4 3.8 %collective-permute-start = (bf16[256,1024]{1,0:T(8,128)(2,1)}, bf16[256,1024]{1,0:T(8,128)(2,1)S(1)}, u32[]{:S(2)}, u32[]{:S(2)}) collective-permute-start(bf16[256,1024]{1,0:T(8,128)(2,1)} %get-tuple-element.10), channel_id=1, source_target_pairs={{0,1},{1,2},{2,3},{3,4},{4,5},{5,6},{6,7},{7,8},{8,9},{9,10},{10,1... | collective-permute-start | bytes 1572872 | tf_op jit(solution)/shard_map/ppermute | solution.py:17
  6.2 11.3 %collective-permute-start.1 = (bf16[256,1024]{1,0:T(8,128)(2,1)}, bf16[256,1024]{1,0:T(8,128)(2,1)}, u32[]{:S(2)}, u32[]{:S(2)}) collective-permute-start(bf16[256,1024]{1,0:T(8,128)(2,1)} %get-tuple-element.11), channel_id=1, source_target_pairs={{1,0},{2,1},{3,2},{4,3},{5,4},{6,5},{7,6},{8,7},{9,8},{10,9},{11,1... | collective-permute-start | bytes 1572872 | tf_op jit(solution)/shard_map/ppermute | solution.py:19
  17.5 1.4 %fusion.18 = (f32[1]{0:T(128)}, f32[1]{0:T(128)}) fusion(f32[2]{0:T(128)} %param.9), kind=kLoop, calls=%fused_computation.30 | loop fusion | bytes 16 | tf_op jit(solution)/shard_map/slice | solution.py:32
  21.4 0.7 compare_and_fusion
  22.1 0.1 reshape.47
  22.2 5.2 %collective-permute-done = bf16[256,1024]{1,0:T(8,128)(2,1)S(1)} collective-permute-done((bf16[256,1024]{1,0:T(8,128)(2,1)}, bf16[256,1024]{1,0:T(8,128)(2,1)S(1)}, u32[]{:S(2)}, u32[]{:S(2)}) %collective-permute-start) | collective-permute-done | bytes 524320 | tf_op jit(solution)/shard_map/ppermute | solution.py:17
  27.4 1.2 %collective-permute-done.1 = bf16[256,1024]{1,0:T(8,128)(2,1)} collective-permute-done((bf16[256,1024]{1,0:T(8,128)(2,1)}, bf16[256,1024]{1,0:T(8,128)(2,1)}, u32[]{:S(2)}, u32[]{:S(2)}) %collective-permute-start.1) | collective-permute-done | bytes 524320 | tf_op jit(solution)/shard_map/ppermute | solution.py:19
  28.7 2.8 %pad_maximum_fusion = bf16[1280,1024]{1,0:T(8,128)(2,1)} fusion(bf16[256,1024]{1,0:T(8,128)(2,1)} %collective-permute-done.1, bf16[768,1024]{1,0:T(8,128)(2,1)S(1)} %copy-done.1, bf16[256,1024]{1,0:T(8,128)(2,1)S(1)} %collective-permute-done), kind=kLoop, calls=%fused_computation.19 | loop fusion | flops 7864320 | bytes 5242880 | tf_op jit(solution)/shard_map/concatenate | solution.py:15
  31.5 6.6 %gather_fusion = bf16[30,128,1024]{2,1,0:T(8,128)(2,1)} fusion(bf16[10,128,1024]{2,1,0:T(8,128)(2,1)} %bitcast.29, s32[1024]{0:T(1024)S(1)} %pad_clamp_fusion), kind=kCustom, calls=%fused_computation.clone | custom fusion | bytes 15728760 | tf_op jit(solution)/shard_map/jit(_take)/gather | solution.py:40
  38.1 4.8 %fusion.2 = f32[6,1024,128,1]{1,2,3,0:T(8,128)S(1)} fusion(bf16[6,5,128,128]{3,2,1,0:T(8,128)(2,1)S(1)} %copy-done, bf16[6,5,128,1024]{3,2,1,0:T(8,128)(2,1)} %bitcast.31, pred[6,5]{1,0:T(8,128)(4,1)S(1)} %get-tuple-element.6), kind=kOutput, calls=%fused_computation.4 | convolution fusion | flops 1010565120 | bytes 11993118 | tf_op jit(solution)/shard_map/rkij,rkjm->rim/dot_general | solution.py:41
  42.9 0.7 fusion.10
  43.5 0.0 copy-start.2
  43.6 0.1 fusion.16
  43.6 1.9 %collective-permute-start.2 = (bf16[256,1024]{1,0:T(8,128)(2,1)S(1)}, bf16[256,1024]{1,0:T(8,128)(2,1)S(1)}, u32[]{:S(2)}, u32[]{:S(2)}) collective-permute-start(bf16[256,1024]{1,0:T(8,128)(2,1)S(1)} %get-tuple-element.8), channel_id=1, source_target_pairs={{0,1},{1,2},{2,3},{3,4},{4,5},{5,6},{6,7},{7,8},{8,9},{9,10},{10,1... | collective-permute-start | bytes 1572872 | tf_op jit(solution)/shard_map/ppermute | solution.py:17
  45.6 8.1 %collective-permute-start.3 = (bf16[256,1024]{1,0:T(8,128)(2,1)S(1)}, bf16[256,1024]{1,0:T(8,128)(2,1)S(1)}, u32[]{:S(2)}, u32[]{:S(2)}) collective-permute-start(bf16[256,1024]{1,0:T(8,128)(2,1)S(1)} %get-tuple-element.9), channel_id=1, source_target_pairs={{1,0},{2,1},{3,2},{4,3},{5,4},{6,5},{7,6},{8,7},{9,8},{10,9},{11,1... | collective-permute-start | bytes 1572872 | tf_op jit(solution)/shard_map/ppermute | solution.py:19
  53.7 10.1 %collective-permute-done.2 = bf16[256,1024]{1,0:T(8,128)(2,1)S(1)} collective-permute-done((bf16[256,1024]{1,0:T(8,128)(2,1)S(1)}, bf16[256,1024]{1,0:T(8,128)(2,1)S(1)}, u32[]{:S(2)}, u32[]{:S(2)}) %collective-permute-start.2) | collective-permute-done | bytes 524320 | tf_op jit(solution)/shard_map/ppermute | solution.py:17
  63.7 0.0 collective-permute-done.3
  63.7 1.8 %pad_maximum_fusion.1 = bf16[1280,1024]{1,0:T(8,128)(2,1)} fusion(bf16[256,1024]{1,0:T(8,128)(2,1)S(1)} %collective-permute-done.3, bf16[768,1024]{1,0:T(8,128)(2,1)S(1)} %fusion.10, bf16[256,1024]{1,0:T(8,128)(2,1)S(1)} %collective-permute-done.2), kind=kLoop, calls=%fused_computation.20 | loop fusion | flops 7864320 | bytes 5242880 | tf_op jit(solution)/shard_map/concatenate | solution.py:15
  65.6 6.6 %gather_fusion.1 = bf16[30,128,1024]{2,1,0:T(8,128)(2,1)} fusion(bf16[10,128,1024]{2,1,0:T(8,128)(2,1)} %bitcast.28, s32[1024]{0:T(1024)S(1)} %pad_clamp_fusion), kind=kCustom, calls=%fused_computation.1.clone | custom fusion | bytes 15728760 | tf_op jit(solution)/shard_map/jit(_take)/gather | solution.py:40
  72.1 4.9 %fusion = f32[6,1024,128,1]{1,2,3,0:T(8,128)S(1)} fusion(bf16[6,5,128,128]{3,2,1,0:T(8,128)(2,1)S(1)} %copy-done, bf16[6,5,128,1024]{3,2,1,0:T(8,128)(2,1)} %bitcast.30, pred[6,5]{1,0:T(8,128)(4,1)S(1)} %get-tuple-element.6), kind=kOutput, calls=%fused_computation.2 | convolution fusion | flops 1010565120 | bytes 11993118 | tf_op jit(solution)/shard_map/rkij,rkjm->rim/dot_general | solution.py:41
  77.1 0.0 copy-done.3
  77.1 2.1 %fusion.11 = bf16[768,1024]{1,0:T(8,128)(2,1)} fusion(bf16[768,1024]{1,0:T(8,128)(2,1)S(1)} %copy-done.1, f32[6,1024,128,1]{1,2,3,0:T(8,128)S(1)} %fusion, bf16[768,1024]{1,0:T(8,128)(2,1)S(1)} %copy-done.3, f32[]{:T(128)} %bitcast.7, f32[]{:T(128)} %bitcast.6), kind=kLoop, calls=%fused_computation.15 | loop fusion | flops 6291456 | bytes 7864328 | tf_op jit(solution)/shard_map/convert_element_type | solution.py:50
  (6 shorter events, 0.0 us)
Async XLA Ops:
  0.0 38.1 %copy-start = (bf16[6,5,128,128]{3,2,1,0:T(8,128)(2,1)S(1)}, bf16[6,5,128,128]{3,2,1,0:T(8,128)(2,1)}, u32[]{:S(2)}) copy-start(bf16[6,5,128,128]{3,2,1,0:T(8,128)(2,1)} %param.7) | copy-start | bytes 2949124
  0.0 28.7 %copy-start.1 = (bf16[768,1024]{1,0:T(8,128)(2,1)S(1)}, bf16[768,1024]{1,0:T(8,128)(2,1)}, u32[]{:S(2)}) copy-start(bf16[768,1024]{1,0:T(8,128)(2,1)} %param.6) | copy-start | bytes 4718596
  2.4 25.1 %collective-permute-start = (bf16[256,1024]{1,0:T(8,128)(2,1)}, bf16[256,1024]{1,0:T(8,128)(2,1)S(1)}, u32[]{:S(2)}, u32[]{:S(2)}) collective-permute-start(bf16[256,1024]{1,0:T(8,128)(2,1)} %get-tuple-element.10), channel_id=1, source_target_pairs={{0,1},{1,2},{2,3},{3,4},{4,5},{5,6},{6,7},{7,8},{8,9},{9,10},{10,1... | collective-permute-start | bytes 1572872 | tf_op jit(solution)/shard_map/ppermute | solution.py:17
  6.2 22.5 %collective-permute-start.1 = (bf16[256,1024]{1,0:T(8,128)(2,1)}, bf16[256,1024]{1,0:T(8,128)(2,1)}, u32[]{:S(2)}, u32[]{:S(2)}) collective-permute-start(bf16[256,1024]{1,0:T(8,128)(2,1)} %get-tuple-element.11), channel_id=1, source_target_pairs={{1,0},{2,1},{3,2},{4,3},{5,4},{6,5},{7,6},{8,7},{9,8},{10,9},{11,1... | collective-permute-start | bytes 1572872 | tf_op jit(solution)/shard_map/ppermute | solution.py:19
  43.5 22.0 %copy-start.2 = (bf16[768,1024]{1,0:T(8,128)(2,1)}, bf16[768,1024]{1,0:T(8,128)(2,1)S(1)}, u32[]{:S(2)}) copy-start(bf16[768,1024]{1,0:T(8,128)(2,1)S(1)} %fusion.10) | copy-start | bytes 4718596
  43.6 20.1 %collective-permute-start.2 = (bf16[256,1024]{1,0:T(8,128)(2,1)S(1)}, bf16[256,1024]{1,0:T(8,128)(2,1)S(1)}, u32[]{:S(2)}, u32[]{:S(2)}) collective-permute-start(bf16[256,1024]{1,0:T(8,128)(2,1)S(1)} %get-tuple-element.8), channel_id=1, source_target_pairs={{0,1},{1,2},{2,3},{3,4},{4,5},{5,6},{6,7},{7,8},{8,9},{9,10},{10,1... | collective-permute-start | bytes 1572872 | tf_op jit(solution)/shard_map/ppermute | solution.py:17
  45.6 18.2 %collective-permute-start.3 = (bf16[256,1024]{1,0:T(8,128)(2,1)S(1)}, bf16[256,1024]{1,0:T(8,128)(2,1)S(1)}, u32[]{:S(2)}, u32[]{:S(2)}) collective-permute-start(bf16[256,1024]{1,0:T(8,128)(2,1)S(1)} %get-tuple-element.9), channel_id=1, source_target_pairs={{1,0},{2,1},{3,2},{4,3},{5,4},{6,5},{7,6},{8,7},{9,8},{10,9},{11,1... | collective-permute-start | bytes 1572872 | tf_op jit(solution)/shard_map/ppermute | solution.py:19
  72.1 4.9 %copy-start.3 = (bf16[768,1024]{1,0:T(8,128)(2,1)S(1)}, bf16[768,1024]{1,0:T(8,128)(2,1)}, u32[]{:S(2)}) copy-start(bf16[768,1024]{1,0:T(8,128)(2,1)} %copy-done.2) | copy-start | bytes 4718596
where the time goes:
time: 79.6 us; the launch traced here: 79.2 us
  starting transfers between devices  25.1 us (32%)
  local copies, waits for them, and re-layouts  17 us (21%)
  waiting for transfers between devices  16.5 us (21%)
  matrix products  9.74 us (12%)
  other arithmetic  8.11 us (10%)
  between operations  2.61 us (3%)
    ppermute x2, starting transfers between devices, extended(): lax.ppermute(head, axis, [((i + 1) % count, i) for i in range(count)])  19.4 us
    ppermute x2, waiting for transfers between devices, extended(): lax.ppermute(tail, axis, [(i, (i + 1) % count) for i in range(count)])  15.3 us
    gather x2, local copies, waits for them, and re-layouts, per_device(): picked = jnp.take(grid, local_index, axis=0)  13.1 us
    dot_general x2, matrix products, per_device(): jnp.einsum('rkij,rkjm->rim', ham_blocks, picked, preferred_element_type=j...  9.74 us
    ppermute x2, starting transfers between devices, extended(): lax.ppermute(tail, axis, [(i, (i + 1) % count) for i in range(count)])  5.73 us
    concatenate x2, other arithmetic, extended(): jnp.concatenate([lax.ppermute(tail, axis, [(i, (i + 1) % count) for i in...  4.64 us
    convert_element_type x2, other arithmetic, per_device(): previous, current = (current, updated.astype(jnp.bfloat16))  2.75 us
    slice x2, local copies, waits for them, and re-layouts, extended(): lax.slice_in_dim(cells, cells.shape[dim] - width, cells.shape[dim], axis=...  2.44 us
  transfers between devices with their start and end apart: 4, of which 3 were waited for; matrix products, arithmetic and copies ran while one was open for 3% of the time, Pallas kernels for 0%

commit v1 on v0

v1 whole, which is shorter than its diff:
```python
import functools

import jax
import jax.numpy as jnp
from jax import lax
from jax.experimental import pallas as pl
from jax.experimental.pallas import tpu as pltpu
from jax.sharding import PartitionSpec as P

REACH = 2
MESH = pl.DeviceIdType.MESH
F32 = jnp.float32
BF16 = jnp.bfloat16
CHUNKS = 4


def dot(a, b):
    return jnp.dot(a, b, preferred_element_type=F32)


def kernel(
    rows_n, cols_n, chunks,
    bounds_ref, columns_ref, vec_hbm, ham_hbm, out_hbm,
    ham, band, turned, vec, halo, part_send, part_own, part_far, first, image, result,
    load_sem, ham_sem, send_sem, recv_sem, out_sem,
):
    here = ham.shape[0]
    slots = ham.shape[1]
    block = ham.shape[2]
    side = REACH * block
    height = here * block
    width = vec.shape[2]
    last = height - side
    devices = rows_n * cols_n
    blocks_all = devices * here
    me = lax.axis_index("row") * cols_n + lax.axis_index("col")
    after = lax.rem(me + 1, devices)
    before = lax.rem(me + devices - 1, devices)
    right = (after // cols_n, lax.rem(after, cols_n))
    left = (before // cols_n, lax.rem(before, cols_n))

    barrier = pltpu.get_barrier_semaphore()
    for other in (left, right):
        pl.semaphore_signal(barrier, inc=1, device_id=other, device_id_type=MESH)

    def lanes(c):
        return pl.ds(pl.multiple_of(c * width, width), width)

    def load(c):
        return pltpu.make_async_copy(vec_hbm.at[:, lanes(c)], vec.at[c], load_sem.at[c])

    def send(kind, c):
        if kind < 2:
            src = vec.at[c, pl.ds(last * kind, side)]
        else:
            src = part_send.at[kind - 2, c]
        return pltpu.make_async_remote_copy(
            src_ref=src,
            dst_ref=halo.at[kind, c],
            send_sem=send_sem.at[kind, c],
            recv_sem=recv_sem.at[kind, c],
            device_id=left if kind % 2 == 0 else right,
            device_id_type=MESH,
        )

    def put(which, c):
        rows = ((0, side), (last, side), (side, height - 2 * side))[which]
        return pltpu.make_async_copy(
            result.at[c, pl.ds(*rows)], out_hbm.at[pl.ds(*rows), lanes(c)], out_sem.at[which, c]
        )

    @pl.loop(0, chunks)
    def _(c):
        load(c).start()

    ham_copy = pltpu.make_async_copy(ham_hbm, ham, ham_sem)
    ham_copy.start()

    @pl.loop(0, chunks)
    def _(c):
        load(c).wait()

    pl.semaphore_wait(barrier, 2)

    @pl.loop(0, chunks)
    def _(c):
        send(0, c).start()
        send(1, c).start()

    ham_copy.wait()
    band[...] = jnp.zeros_like(band)

    @pl.loop(0, here)
    def _(r):
        held = [ham[r, k].astype(F32) for k in range(slots)]
        for offset in range(2 * REACH + 1):
            place = r + offset
            target = lax.rem(me * here + place - REACH + blocks_all, blocks_all)
            total = None
            for k in range(slots):
                term = held[k] * jnp.where(columns_ref[r, k] == target, 1.0, 0.0)
                total = term if total is None else total + term
            band[
                pl.ds(pl.multiple_of(r * block, block), block),
                pl.ds(pl.multiple_of(place * block, block), block),
            ] = total.astype(BF16)

    turned[0] = band[pl.ds(0, side), pl.ds(0, side)].astype(F32).T.astype(BF16)
    turned[1] = band[pl.ds(last, side), pl.ds(height + side, side)].astype(F32).T.astype(BF16)

    low, high = bounds_ref[0], bounds_ref[1]
    center = jnp.full((1, width), 0.5 * (high + low), F32)
    inverse = 1.0 / jnp.full((1, width), 0.5 * (high - low), F32)

    top, bottom = pl.ds(0, side), pl.ds(last, side)
    middle = pl.ds(side, height - 2 * side)
    upper, lower = pl.ds(0, height - side), pl.ds(side, height - side)
    all_in = pl.ds(side, height)
    upper_in, lower_in = pl.ds(side, height - side), pl.ds(2 * side, height - side)

    @pl.loop(0, chunks)
    def _(c):
        top_part = (
            dot(band[top, upper_in], vec[c, upper]) - center * vec[c, top].astype(F32)
        ) * inverse
        part_own[0, c] = top_part
        part_send[0, c] = top_part.astype(BF16)
        bottom_part = (
            dot(band[bottom, lower_in], vec[c, lower]) - center * vec[c, bottom].astype(F32)
        ) * inverse
        part_own[1, c] = bottom_part
        part_send[1, c] = bottom_part.astype(BF16)

    @pl.loop(0, chunks)
    def _(c):
        part_far[0, c] = dot(turned[0], vec[c, top]) * inverse
        part_far[1, c] = dot(turned[1], vec[c, bottom]) * inverse
        send(2, c).start()
        send(3, c).start()
        first[c, middle] = (
            (dot(band[middle, all_in], vec[c]) - center * vec[c, middle].astype(F32)) * inverse
        ).astype(BF16)

    @pl.loop(0, chunks)
    def _(c):
        send(1, c).wait_recv()
        first[c, top] = (
            part_own[0, c] + dot(band[top, pl.ds(0, side)], halo[1, c]) * inverse
        ).astype(BF16)
        send(0, c).wait_recv()
        first[c, bottom] = (
            part_own[1, c] + dot(band[bottom, pl.ds(height + side, side)], halo[0, c]) * inverse
        ).astype(BF16)
        result[c, middle] = (
            2.0 * (
                (dot(band[middle, all_in], first[c]) - center * first[c, middle].astype(F32))
                * inverse
            )
            - vec[c, middle].astype(F32)
        ).astype(BF16)
        put(2, c).start()
        image[0, c] = dot(band[top, upper_in], first[c, upper]) - center * first[
            c, top
        ].astype(F32)
        image[1, c] = dot(band[bottom, lower_in], first[c, lower]) - center * first[
            c, bottom
        ].astype(F32)

    @pl.loop(0, chunks)
    def _(c):
        send(3, c).wait_recv()
        beyond = (halo[3, c].astype(F32) + part_far[0, c]).astype(BF16)
        result[c, top] = (
            2.0 * ((image[0, c] + dot(band[top, pl.ds(0, side)], beyond)) * inverse)
            - vec[c, top].astype(F32)
        ).astype(BF16)
        put(0, c).start()
        send(2, c).wait_recv()
        beyond = (halo[2, c].astype(F32) + part_far[1, c]).astype(BF16)
        result[c, bottom] = (
            2.0 * (
                (image[1, c] + dot(band[bottom, pl.ds(height + side, side)], beyond)) * inverse
            )
            - vec[c, bottom].astype(F32)
        ).astype(BF16)
        put(1, c).start()

    @pl.loop(0, chunks)
    def _(c):
        for kind in range(4):
            send(kind, c).wait_send()
        for which in range(3):
            put(which, c).wait()


def per_device(rows_n, cols_n, vectors, ham_blocks, ham_columns, bounds):
    height, vec_width = vectors.shape
    here, slots, block, _ = ham_blocks.shape
    side = REACH * block
    chunks = CHUNKS
    width = vec_width // chunks
    return pl.pallas_call(
        functools.partial(kernel, rows_n, cols_n, chunks),
        out_shape=jax.ShapeDtypeStruct((height, vec_width), BF16),
        in_specs=[
            pl.BlockSpec(memory_space=pltpu.SMEM),
            pl.BlockSpec(memory_space=pltpu.SMEM),
            pl.BlockSpec(memory_space=pl.ANY),
            pl.BlockSpec(memory_space=pl.ANY),
        ],
        out_specs=pl.BlockSpec(memory_space=pl.ANY),
        scratch_shapes=[
            pltpu.VMEM((here, slots, block, block), BF16),
            pltpu.VMEM((height, height + 2 * side), BF16),
            pltpu.VMEM((2, side, side), BF16),
            pltpu.VMEM((chunks, height, width), BF16),
            pltpu.VMEM((4, chunks, side, width), BF16),
            pltpu.VMEM((2, chunks, side, width), BF16),
            pltpu.VMEM((2, chunks, side, width), F32),
            pltpu.VMEM((2, chunks, side, width), F32),
            pltpu.VMEM((chunks, height, width), BF16),
            pltpu.VMEM((2, chunks, side, width), F32),
            pltpu.VMEM((chunks, height, width), BF16),
            pltpu.SemaphoreType.DMA((chunks,)),
            pltpu.SemaphoreType.DMA,
            pltpu.SemaphoreType.DMA((4, chunks)),
            pltpu.SemaphoreType.DMA((4, chunks)),
            pltpu.SemaphoreType.DMA((3, chunks)),
        ],
        compiler_params=pltpu.CompilerParams(collective_id=0, has_side_effects=True),
    )(bounds, ham_columns, vectors, ham_blocks)


def solution(mesh):
    return jax.shard_map(
        functools.partial(per_device, mesh.shape["row"], mesh.shape["col"]),
        mesh=mesh,
        in_specs=(
            P(("row", "col"), None),
            P(("row", "col"), None, None, None),
            P(("row", "col"), None),
            P(),
        ),
        out_specs=P(("row", "col"), None),
        check_vma=False,
    )
```

time: 79.6 us -> 41.9 us (0.53)
  the two profiles are of different devices: /device:TPU:24 before, /device:TPU:1 now
where the time goes in v1:
time: 41.9 us; the launch traced here: 41.7 us
  Pallas kernels  39.1 us (93%)
  local copies, waits for them, and re-layouts  2.67 us (6%)
    pallas_call x1, Pallas kernels, per_device(): pl.pallas_call(functools.partial(kernel, rows_n, cols_n, chunks), out_sha...  39.1 us
    unnamed x1, local copies, waits for them, and re-layouts  2.67 us

profile of v1, /device:TPU:1, one launch (start us, length us, event | category | flops | bytes accessed | tf_op | source)
XLA Modules:
  0.0 41.7 jit_solution(1780250190638008873)
XLA Ops:
  0.0 39.1 %shard_map.46 = bf16[768,1024]{1,0:T(8,128)(2,1)} custom-call(f32[2]{0:T(128)} %bounds_ref.1, s32[6,5]{1,0:T(8,128)} %columns_ref.1, bf16[768,1024]{1,0:T(8,128)(2,1)} %vec_hbm.1, bf16[6,5,128,128]{3,2,1,0:T(8,128)(2,1)} %ham_hbm.1), custom_call_target="tpu_custom_call" | custom-call | tf_op jit(solution)/shard_map/pallas_call | solution.py:202
  39.1 2.7 %copy.6 = bf16[768,1024]{1,0:T(8,128)(2,1)} copy(bf16[768,1024]{1,0:T(8,128)(2,1)} %shard_map.46) | data formatting | bytes 3145728

commit v2 on v1

--- a/solution.py
+++ b/solution.py
@@ -12,6 +12,7 @@
 F32 = jnp.float32
 BF16 = jnp.bfloat16
 CHUNKS = 4
+VMEM_BYTES = 20 << 20
 
 
 def dot(a, b):
@@ -20,9 +21,9 @@
 
 def kernel(
     rows_n, cols_n, chunks,
-    bounds_ref, columns_ref, vec_hbm, ham_hbm, out_hbm,
-    ham, band, turned, vec, halo, part_send, part_own, part_far, first, image, result,
-    load_sem, ham_sem, send_sem, recv_sem, out_sem,
+    bounds_ref, columns_ref, vec_hbm, ham_hbm, out_ref,
+    ham, band, turned, vec, halo, part_send, part_own, part_far, first, image,
+    load_sem, ham_sem, send_sem, recv_sem,
 ):
     here = ham.shape[0]
     slots = ham.shape[1]
@@ -51,7 +52,7 @@
 
     def send(kind, c):
         if kind < 2:
-            src = vec.at[c, pl.ds(last * kind, side)]
+            src = vec_hbm.at[pl.ds(last * kind, side), lanes(c)]
         else:
             src = part_send.at[kind - 2, c]
         return pltpu.make_async_remote_copy(
@@ -63,22 +64,12 @@
             device_id_type=MESH,
         )
 
-    def put(which, c):
-        rows = ((0, side), (last, side), (side, height - 2 * side))[which]
-        return pltpu.make_async_copy(
-            result.at[c, pl.ds(*rows)], out_hbm.at[pl.ds(*rows), lanes(c)], out_sem.at[which, c]
-        )
-
-    @pl.loop(0, chunks)
-    def _(c):
-        load(c).start()
-
     ham_copy = pltpu.make_async_copy(ham_hbm, ham, ham_sem)
     ham_copy.start()
 
     @pl.loop(0, chunks)
     def _(c):
-        load(c).wait()
+        load(c).start()
 
     pl.semaphore_wait(barrier, 2)
 
@@ -120,6 +111,7 @@
 
     @pl.loop(0, chunks)
     def _(c):
+        load(c).wait()
         top_part = (
             dot(band[top, upper_in], vec[c, upper]) - center * vec[c, top].astype(F32)
         ) * inverse
@@ -151,14 +143,13 @@
         first[c, bottom] = (
             part_own[1, c] + dot(band[bottom, pl.ds(height + side, side)], halo[0, c]) * inverse
         ).astype(BF16)
-        result[c, middle] = (
+        out_ref[middle, lanes(c)] = (
             2.0 * (
                 (dot(band[middle, all_in], first[c]) - center * first[c, middle].astype(F32))
                 * inverse
             )
             - vec[c, middle].astype(F32)
         ).astype(BF16)
-        put(2, c).start()
         image[0, c] = dot(band[top, upper_in], first[c, upper]) - center * first[
             c, top
         ].astype(F32)
@@ -170,27 +161,23 @@
     def _(c):
         send(3, c).wait_recv()
         beyond = (halo[3, c].astype(F32) + part_far[0, c]).astype(BF16)
-        result[c, top] = (
+        out_ref[top, lanes(c)] = (
             2.0 * ((image[0, c] + dot(band[top, pl.ds(0, side)], beyond)) * inverse)
             - vec[c, top].astype(F32)
         ).astype(BF16)
-        put(0, c).start()
         send(2, c).wait_recv()
         beyond = (halo[2, c].astype(F32) + part_far[1, c]).astype(BF16)
-        result[c, bottom] = (
+        out_ref[bottom, lanes(c)] = (
             2.0 * (
                 (image[1, c] + dot(band[bottom, pl.ds(height + side, side)], beyond)) * inverse
             )
             - vec[c, bottom].astype(F32)
         ).astype(BF16)
-        put(1, c).start()
 
     @pl.loop(0, chunks)
     def _(c):
         for kind in range(4):
             send(kind, c).wait_send()
-        for which in range(3):
-            put(which, c).wait()
 
 
 def per_device(rows_n, cols_n, vectors, ham_blocks, ham_columns, bounds):
@@ -205,10 +192,10 @@
         in_specs=[
             pl.BlockSpec(memory_space=pltpu.SMEM),
             pl.BlockSpec(memory_space=pltpu.SMEM),
-            pl.BlockSpec(memory_space=pl.ANY),
-            pl.BlockSpec(memory_space=pl.ANY),
+            pl.BlockSpec(memory_space=pltpu.HBM),
+            pl.BlockSpec(memory_space=pltpu.HBM),
         ],
-        out_specs=pl.BlockSpec(memory_space=pl.ANY),
+        out_specs=pl.BlockSpec(memory_space=pltpu.VMEM),
         scratch_shapes=[
             pltpu.VMEM((here, slots, block, block), BF16),
             pltpu.VMEM((height, height + 2 * side), BF16),
@@ -220,15 +207,15 @@
             pltpu.VMEM((2, chunks, side, width), F32),
             pltpu.VMEM((chunks, height, width), BF16),
             pltpu.VMEM((2, chunks, side, width), F32),
-            pltpu.VMEM((chunks, height, width), BF16),
             pltpu.SemaphoreType.DMA((chunks,)),
             pltpu.SemaphoreType.DMA,
             pltpu.SemaphoreType.DMA((4, chunks)),
             pltpu.SemaphoreType.DMA((4, chunks)),
-            pltpu.SemaphoreType.DMA((3, chunks)),
         ],
-        compiler_params=pltpu.CompilerParams(collective_id=0, has_side_effects=True),
-    )(bounds, ham_columns, vectors, ham_blocks)
+        compiler_params=pltpu.CompilerParams(
+            collective_id=0, has_side_effects=True, vmem_limit_bytes=VMEM_BYTES
+        ),
+    )(*[pltpu.with_memory_space_constraint(a, pltpu.HBM) for a in (bounds, ham_columns, vectors, ham_blocks)])
 
 
 def solution(mesh):

time: 41.9 us -> 39.2 us (0.936)
  local copies, waits for them, and re-layouts: 2.67 us -> 1.15 us
  Pallas kernels: 39.1 us -> 37.9 us
    unnamed x1, local copies, waits for them, and re-layouts: 2.67 us -> 1.15 us
    pallas_call x1, Pallas kernels: 39.1 us -> 37.9 us  [per_device(): pl.pallas_call(functools.partial(kernel, rows_n, cols_n, chunks), out_sha...]
where the time goes in v2:
time: 39.2 us; the launch traced here: 39 us
  Pallas kernels  37.9 us (97%)
  local copies, waits for them, and re-layouts  1.15 us (3%)
    pallas_call x1, Pallas kernels, per_device(): pl.pallas_call(functools.partial(kernel, rows_n, cols_n, chunks), out_sha...  37.9 us
    unnamed x1, local copies, waits for them, and re-layouts  1.15 us

profile of v2, /device:TPU:1, one launch (start us, length us, event | category | flops | bytes accessed | tf_op | source)
XLA Modules:
  0.0 39.0 jit_solution(11952234193735031939)
XLA Ops:
  0.0 37.9 %shard_map.46 = bf16[768,1024]{1,0:T(8,128)(2,1)S(1)} custom-call(f32[2]{0:T(128)} %bounds_ref.1, s32[6,5]{1,0:T(8,128)} %columns_ref.1, bf16[768,1024]{1,0:T(8,128)(2,1)} %vec_hbm.1, bf16[6,5,128,128]{3,2,1,0:T(8,128)(2,1)} %ham_hbm.1), custom_call_target="tpu_custom_call" | custom-call | tf_op jit(solution)/shard_map/pallas_call | solution.py:189
  37.9 1.1 %copy.6 = bf16[768,1024]{1,0:T(8,128)(2,1)} copy(bf16[768,1024]{1,0:T(8,128)(2,1)S(1)} %shard_map.46) | data formatting | bytes 3145728

commit v3 on v2

--- a/solution.py
+++ b/solution.py
@@ -21,9 +21,9 @@
 
 def kernel(
     rows_n, cols_n, chunks,
-    bounds_ref, columns_ref, vec_hbm, ham_hbm, out_ref,
-    ham, band, turned, vec, halo, part_send, part_own, part_far, first, image,
-    load_sem, ham_sem, send_sem, recv_sem,
+    bounds_hbm, columns_hbm, vec_hbm, ham_hbm, out_ref,
+    bounds_ref, columns_ref, ham, band, turned, vec, halo, part_send, part_own, part_far, first, image,
+    load_sem, ham_sem, small_sem, send_sem, recv_sem,
 ):
     here = ham.shape[0]
     slots = ham.shape[1]
@@ -64,6 +64,12 @@
             device_id_type=MESH,
         )
 
+    small = [
+        pltpu.make_async_copy(columns_hbm, columns_ref, small_sem.at[0]),
+        pltpu.make_async_copy(bounds_hbm, bounds_ref, small_sem.at[1]),
+    ]
+    for copy in small:
+        copy.start()
     ham_copy = pltpu.make_async_copy(ham_hbm, ham, ham_sem)
     ham_copy.start()
 
@@ -78,6 +84,8 @@
         send(0, c).start()
         send(1, c).start()
 
+    for copy in small:
+        copy.wait()
     ham_copy.wait()
     band[...] = jnp.zeros_like(band)
 
@@ -102,6 +110,7 @@
     low, high = bounds_ref[0], bounds_ref[1]
     center = jnp.full((1, width), 0.5 * (high + low), F32)
     inverse = 1.0 / jnp.full((1, width), 0.5 * (high - low), F32)
+    double = 2.0 * inverse
 
     top, bottom = pl.ds(0, side), pl.ds(last, side)
     middle = pl.ds(side, height - 2 * side)
@@ -144,34 +153,27 @@
             part_own[1, c] + dot(band[bottom, pl.ds(height + side, side)], halo[0, c]) * inverse
         ).astype(BF16)
         out_ref[middle, lanes(c)] = (
-            2.0 * (
-                (dot(band[middle, all_in], first[c]) - center * first[c, middle].astype(F32))
-                * inverse
-            )
+            (dot(band[middle, all_in], first[c]) - center * first[c, middle].astype(F32)) * double
             - vec[c, middle].astype(F32)
         ).astype(BF16)
-        image[0, c] = dot(band[top, upper_in], first[c, upper]) - center * first[
-            c, top
-        ].astype(F32)
-        image[1, c] = dot(band[bottom, lower_in], first[c, lower]) - center * first[
-            c, bottom
-        ].astype(F32)
-
-    @pl.loop(0, chunks)
-    def _(c):
+        image[0, c] = (
+            dot(band[top, upper_in], first[c, upper]) - center * first[c, top].astype(F32)
+        ) * double - vec[c, top].astype(F32)
+        image[1, c] = (
+            dot(band[bottom, lower_in], first[c, lower]) - center * first[c, bottom].astype(F32)
+        ) * double - vec[c, bottom].astype(F32)
+
+    @pl.loop(0, chunks)
+    def _(c):
+        send(2, c).wait_recv()
+        beyond = (halo[2, c].astype(F32) + part_far[1, c]).astype(BF16)
+        out_ref[bottom, lanes(c)] = (
+            image[1, c] + dot(band[bottom, pl.ds(height + side, side)], beyond) * double
+        ).astype(BF16)
         send(3, c).wait_recv()
         beyond = (halo[3, c].astype(F32) + part_far[0, c]).astype(BF16)
         out_ref[top, lanes(c)] = (
-            2.0 * ((image[0, c] + dot(band[top, pl.ds(0, side)], beyond)) * inverse)
-            - vec[c, top].astype(F32)
-        ).astype(BF16)
-        send(2, c).wait_recv()
-        beyond = (halo[2, c].astype(F32) + part_far[1, c]).astype(BF16)
-        out_ref[bottom, lanes(c)] = (
-            2.0 * (
-                (image[1, c] + dot(band[bottom, pl.ds(height + side, side)], beyond)) * inverse
-            )
-            - vec[c, bottom].astype(F32)
+            image[0, c] + dot(band[top, pl.ds(0, side)], beyond) * double
         ).astype(BF16)
 
     @pl.loop(0, chunks)
@@ -190,13 +192,15 @@
         functools.partial(kernel, rows_n, cols_n, chunks),
         out_shape=jax.ShapeDtypeStruct((height, vec_width), BF16),
         in_specs=[
-            pl.BlockSpec(memory_space=pltpu.SMEM),
-            pl.BlockSpec(memory_space=pltpu.SMEM),
+            pl.BlockSpec(memory_space=pltpu.HBM),
+            pl.BlockSpec(memory_space=pltpu.HBM),
             pl.BlockSpec(memory_space=pltpu.HBM),
             pl.BlockSpec(memory_space=pltpu.HBM),
         ],
         out_specs=pl.BlockSpec(memory_space=pltpu.VMEM),
         scratch_shapes=[
+            pltpu.SMEM(bounds.shape, F32),
+            pltpu.SMEM(ham_columns.shape, jnp.int32),
             pltpu.VMEM((here, slots, block, block), BF16),
             pltpu.VMEM((height, height + 2 * side), BF16),
             pltpu.VMEM((2, side, side), BF16),
@@ -209,6 +213,7 @@
             pltpu.VMEM((2, chunks, side, width), F32),
             pltpu.SemaphoreType.DMA((chunks,)),
             pltpu.SemaphoreType.DMA,
+            pltpu.SemaphoreType.DMA((2,)),
             pltpu.SemaphoreType.DMA((4, chunks)),
             pltpu.SemaphoreType.DMA((4, chunks)),
         ],

time: 39.2 us -> 38.2 us (0.974)
  Pallas kernels: 37.9 us -> 36.9 us
    pallas_call x1, Pallas kernels: 37.9 us -> 36.9 us  [per_device(): pl.pallas_call(functools.partial(kernel, rows_n, cols_n, chunks), out_sha...]
where the time goes in v3:
time: 38.2 us; the launch traced here: 38.1 us
  Pallas kernels  36.9 us (97%)
  local copies, waits for them, and re-layouts  1.15 us (3%)
    pallas_call x1, Pallas kernels, per_device(): pl.pallas_call(functools.partial(kernel, rows_n, cols_n, chunks), out_sha...  36.9 us
    unnamed x1, local copies, waits for them, and re-layouts  1.15 us

profile of v3, /device:TPU:1, one launch (start us, length us, event | category | flops | bytes accessed | tf_op | source)
XLA Modules:
  0.0 38.1 jit_solution(17103465527075223549)
XLA Ops:
  0.0 36.9 %shard_map.46 = bf16[768,1024]{1,0:T(8,128)(2,1)S(1)} custom-call(f32[2]{0:T(128)} %bounds_hbm.1, s32[6,5]{1,0:T(8,128)} %columns_hbm.1, bf16[768,1024]{1,0:T(8,128)(2,1)} %vec_hbm.1, bf16[6,5,128,128]{3,2,1,0:T(8,128)(2,1)} %ham_hbm.1), custom_call_target="tpu_custom_call" | custom-call | tf_op jit(solution)/shard_map/pallas_call | solution.py:191
  37.0 1.1 %copy.6 = bf16[768,1024]{1,0:T(8,128)(2,1)} copy(bf16[768,1024]{1,0:T(8,128)(2,1)S(1)} %shard_map.46) | data formatting | bytes 3145728

commit v4 on v3

--- a/solution.py
+++ b/solution.py
@@ -23,7 +23,7 @@
     rows_n, cols_n, chunks,
     bounds_hbm, columns_hbm, vec_hbm, ham_hbm, out_ref,
     bounds_ref, columns_ref, ham, band, turned, vec, halo, part_send, part_own, part_far, first, image,
-    load_sem, ham_sem, small_sem, send_sem, recv_sem,
+    load_sem, ham_sem, small_sem, ready_sem, send_sem, recv_sem,
 ):
     here = ham.shape[0]
     slots = ham.shape[1]
@@ -41,8 +41,7 @@
     left = (before // cols_n, lax.rem(before, cols_n))
 
     barrier = pltpu.get_barrier_semaphore()
-    for other in (left, right):
-        pl.semaphore_signal(barrier, inc=1, device_id=other, device_id_type=MESH)
+    pl.semaphore_signal(barrier, inc=1, device_id=left, device_id_type=MESH)
 
     def lanes(c):
         return pl.ds(pl.multiple_of(c * width, width), width)
@@ -64,6 +63,14 @@
             device_id_type=MESH,
         )
 
+    pl.semaphore_wait(barrier, 1)
+
+    @pl.loop(0, chunks)
+    def _(c):
+        send(1, c).start()
+
+    pl.semaphore_signal(ready_sem, inc=1, device_id=right, device_id_type=MESH)
+
     small = [
         pltpu.make_async_copy(columns_hbm, columns_ref, small_sem.at[0]),
         pltpu.make_async_copy(bounds_hbm, bounds_ref, small_sem.at[1]),
@@ -77,12 +84,11 @@
     def _(c):
         load(c).start()
 
-    pl.semaphore_wait(barrier, 2)
+    pl.semaphore_wait(ready_sem, 1)
 
     @pl.loop(0, chunks)
     def _(c):
         send(0, c).start()
-        send(1, c).start()
 
     for copy in small:
         copy.wait()
@@ -214,6 +220,7 @@
             pltpu.SemaphoreType.DMA((chunks,)),
             pltpu.SemaphoreType.DMA,
             pltpu.SemaphoreType.DMA((2,)),
+            pltpu.SemaphoreType.REGULAR,
             pltpu.SemaphoreType.DMA((4, chunks)),
             pltpu.SemaphoreType.DMA((4, chunks)),
         ],

time: 38.2 us -> 37.5 us (0.982)
  Pallas kernels: 36.9 us -> 36.2 us
    pallas_call x1, Pallas kernels: 36.9 us -> 36.2 us  [per_device(): pl.pallas_call(functools.partial(kernel, rows_n, cols_n, chunks), out_sha...]
where the time goes in v4:
time: 37.5 us; the launch traced here: 37.4 us
  Pallas kernels  36.2 us (97%)
  local copies, waits for them, and re-layouts  1.15 us (3%)
    pallas_call x1, Pallas kernels, per_device(): pl.pallas_call(functools.partial(kernel, rows_n, cols_n, chunks), out_sha...  36.2 us
    unnamed x1, local copies, waits for them, and re-layouts  1.15 us

profile of v4, /device:TPU:1, one launch (start us, length us, event | category | flops | bytes accessed | tf_op | source)
XLA Modules:
  0.0 37.4 jit_solution(9826251088191189203)
XLA Ops:
  0.0 36.2 %shard_map.46 = bf16[768,1024]{1,0:T(8,128)(2,1)S(1)} custom-call(f32[2]{0:T(128)} %bounds_hbm.1, s32[6,5]{1,0:T(8,128)} %columns_hbm.1, bf16[768,1024]{1,0:T(8,128)(2,1)} %vec_hbm.1, bf16[6,5,128,128]{3,2,1,0:T(8,128)(2,1)} %ham_hbm.1), custom_call_target="tpu_custom_call" | custom-call | tf_op jit(solution)/shard_map/pallas_call | solution.py:197
  36.2 1.1 %copy.6 = bf16[768,1024]{1,0:T(8,128)(2,1)} copy(bf16[768,1024]{1,0:T(8,128)(2,1)S(1)} %shard_map.46) | data formatting | bytes 3145728

commit v5 on v4

--- a/solution.py
+++ b/solution.py
@@ -12,6 +12,8 @@
 F32 = jnp.float32
 BF16 = jnp.bfloat16
 CHUNKS = 4
+VECTOR_PIECES = 1
+PIECES = (1, 1, 1, 1)
 VMEM_BYTES = 20 << 20
 
 
@@ -20,10 +22,11 @@
 
 
 def kernel(
-    rows_n, cols_n, chunks,
+    rows_n, cols_n, chunks, vector_pieces, partial_pieces,
     bounds_hbm, columns_hbm, vec_hbm, ham_hbm, out_ref,
-    bounds_ref, columns_ref, ham, band, turned, vec, halo, part_send, part_own, part_far, first, image,
-    load_sem, ham_sem, small_sem, ready_sem, send_sem, recv_sem,
+    bounds_ref, columns_ref, ham, band, turned, vec, halo, part_halo, part_send, part_own, part_far, first, image,
+    load_sem, ham_sem, small_sem, ready_sem, turn_sem,
+    vec_send_sem, vec_recv_sem, part_send_sem, part_recv_sem,
 ):
     here = ham.shape[0]
     slots = ham.shape[1]
@@ -31,6 +34,7 @@
     side = REACH * block
     height = here * block
     width = vec.shape[2]
+    total_width = chunks * width
     last = height - side
     devices = rows_n * cols_n
     blocks_all = devices * here
@@ -40,34 +44,57 @@
     right = (after // cols_n, lax.rem(after, cols_n))
     left = (before // cols_n, lax.rem(before, cols_n))
 
+    row, col = lax.axis_index("row"), lax.axis_index("col")
+    run = cols_n // 2
+    core = lax.rem(row, 2)
+    far = lax.rem(row // 2, 2) * (col // run)
+    at_end = (lax.rem(col, run) == run - 1).astype(jnp.int32)
+    leads = at_end * (1 - lax.rem(core + far, 2))
+    follows = at_end - leads
+    partner = (row + 1 - 2 * core, col)
+
+    turn = len(partial_pieces) // 2
+
     barrier = pltpu.get_barrier_semaphore()
     pl.semaphore_signal(barrier, inc=1, device_id=left, device_id_type=MESH)
 
+    @pl.when(follows == 1)
+    def _():
+        pl.semaphore_signal(barrier, inc=1, device_id=partner, device_id_type=MESH)
+
+
     def lanes(c):
         return pl.ds(pl.multiple_of(c * width, width), width)
 
     def load(c):
         return pltpu.make_async_copy(vec_hbm.at[:, lanes(c)], vec.at[c], load_sem.at[c])
 
-    def send(kind, c):
-        if kind < 2:
-            src = vec_hbm.at[pl.ds(last * kind, side), lanes(c)]
-        else:
-            src = part_send.at[kind - 2, c]
+    def send_vectors(kind, k):
+        part = pl.ds(k * (total_width // vector_pieces), total_width // vector_pieces)
         return pltpu.make_async_remote_copy(
-            src_ref=src,
-            dst_ref=halo.at[kind, c],
-            send_sem=send_sem.at[kind, c],
-            recv_sem=recv_sem.at[kind, c],
-            device_id=left if kind % 2 == 0 else right,
+            src_ref=vec_hbm.at[pl.ds(last * kind, side), part],
+            dst_ref=halo.at[kind, :, part],
+            send_sem=vec_send_sem.at[kind, k],
+            recv_sem=vec_recv_sem.at[kind, k],
+            device_id=(left, right)[kind],
             device_id_type=MESH,
         )
 
-    pl.semaphore_wait(barrier, 1)
-
-    @pl.loop(0, chunks)
-    def _(c):
-        send(1, c).start()
+    def send_partial(kind, k):
+        part = pl.ds(*partial_pieces[k])
+        return pltpu.make_async_remote_copy(
+            src_ref=part_send.at[kind, :, part],
+            dst_ref=part_halo.at[kind, :, part],
+            send_sem=part_send_sem.at[kind, k],
+            recv_sem=part_recv_sem.at[kind, k],
+            device_id=(left, right)[kind],
+            device_id_type=MESH,
+        )
+
+    pl.semaphore_wait(barrier, 1 + leads)
+
+    for k in range(vector_pieces):
+        send_vectors(1, k).start()
 
     pl.semaphore_signal(ready_sem, inc=1, device_id=right, device_id_type=MESH)
 
@@ -86,9 +113,8 @@
 
     pl.semaphore_wait(ready_sem, 1)
 
-    @pl.loop(0, chunks)
-    def _(c):
-        send(0, c).start()
+    for k in range(vector_pieces):
+        send_vectors(0, k).start()
 
     for copy in small:
         copy.wait()
@@ -131,61 +157,93 @@
             dot(band[top, upper_in], vec[c, upper]) - center * vec[c, top].astype(F32)
         ) * inverse
         part_own[0, c] = top_part
-        part_send[0, c] = top_part.astype(BF16)
+        part_send[0, :, lanes(c)] = top_part.astype(BF16)
         bottom_part = (
             dot(band[bottom, lower_in], vec[c, lower]) - center * vec[c, bottom].astype(F32)
         ) * inverse
         part_own[1, c] = bottom_part
-        part_send[1, c] = bottom_part.astype(BF16)
+        part_send[1, :, lanes(c)] = bottom_part.astype(BF16)
 
     @pl.loop(0, chunks)
     def _(c):
-        part_far[0, c] = dot(turned[0], vec[c, top]) * inverse
-        part_far[1, c] = dot(turned[1], vec[c, bottom]) * inverse
-        send(2, c).start()
-        send(3, c).start()
+        part_far[0, :, lanes(c)] = dot(turned[0], vec[c, top]) * inverse
+        part_far[1, :, lanes(c)] = dot(turned[1], vec[c, bottom]) * inverse
+
+    for k in range(len(partial_pieces)):
+        send_partial(0, k).start()
+
+    @pl.when(follows == 0)
+    def _():
+        for k in range(len(partial_pieces)):
+            send_partial(1, k).start()
+
+    @pl.loop(0, chunks)
+    def _(c):
         first[c, middle] = (
             (dot(band[middle, all_in], vec[c]) - center * vec[c, middle].astype(F32)) * inverse
         ).astype(BF16)
 
-    @pl.loop(0, chunks)
-    def _(c):
-        send(1, c).wait_recv()
+    @pl.when(leads == 1)
+    def _():
+        for k in range(turn):
+            send_partial(1, k).wait_send()
+        pl.semaphore_signal(turn_sem, inc=1, device_id=partner, device_id_type=MESH)
+
+    @pl.when(follows == 1)
+    def _():
+        pl.semaphore_wait(turn_sem, 1)
+        for k in range(len(partial_pieces)):
+            send_partial(1, k).start()
+
+    def second(c):
         first[c, top] = (
-            part_own[0, c] + dot(band[top, pl.ds(0, side)], halo[1, c]) * inverse
+            part_own[0, c] + dot(band[top, pl.ds(0, side)], halo[1, :, lanes(c)]) * inverse
         ).astype(BF16)
-        send(0, c).wait_recv()
         first[c, bottom] = (
-            part_own[1, c] + dot(band[bottom, pl.ds(height + side, side)], halo[0, c]) * inverse
+            part_own[1, c]
+            + dot(band[bottom, pl.ds(height + side, side)], halo[0, :, lanes(c)]) * inverse
         ).astype(BF16)
         out_ref[middle, lanes(c)] = (
             (dot(band[middle, all_in], first[c]) - center * first[c, middle].astype(F32)) * double
             - vec[c, middle].astype(F32)
         ).astype(BF16)
-        image[0, c] = (
+        image[0, :, lanes(c)] = (
             dot(band[top, upper_in], first[c, upper]) - center * first[c, top].astype(F32)
         ) * double - vec[c, top].astype(F32)
-        image[1, c] = (
+        image[1, :, lanes(c)] = (
             dot(band[bottom, lower_in], first[c, lower]) - center * first[c, bottom].astype(F32)
         ) * double - vec[c, bottom].astype(F32)
 
-    @pl.loop(0, chunks)
-    def _(c):
-        send(2, c).wait_recv()
-        beyond = (halo[2, c].astype(F32) + part_far[1, c]).astype(BF16)
-        out_ref[bottom, lanes(c)] = (
-            image[1, c] + dot(band[bottom, pl.ds(height + side, side)], beyond) * double
-        ).astype(BF16)
-        send(3, c).wait_recv()
-        beyond = (halo[3, c].astype(F32) + part_far[0, c]).astype(BF16)
-        out_ref[top, lanes(c)] = (
-            image[0, c] + dot(band[top, pl.ds(0, side)], beyond) * double
-        ).astype(BF16)
-
-    @pl.loop(0, chunks)
-    def _(c):
-        for kind in range(4):
-            send(kind, c).wait_send()
+    for k in range(vector_pieces):
+        send_vectors(0, k).wait_recv()
+        send_vectors(1, k).wait_recv()
+        pl.loop(k * chunks // vector_pieces, (k + 1) * chunks // vector_pieces)(second)
+
+    for k, piece in enumerate(partial_pieces):
+        part = pl.ds(*piece)
+        scale = jnp.broadcast_to(double[:, :1], (1, piece[1]))
+        for kind, rows, beside in (
+            (0, bottom, pl.ds(height + side, side)),
+            (1, top, pl.ds(0, side)),
+        ):
+            send_partial(kind, k).wait_recv()
+            beyond = part_halo[kind, :, part].astype(F32) + part_far[1 - kind, :, part]
+            out_ref[rows, part] = (
+                image[1 - kind, :, part] + dot(band[rows, beside], beyond.astype(BF16)) * scale
+            ).astype(BF16)
+
+    @pl.when(leads == 0)
+    def _():
+        for k in range(turn):
+            send_partial(1, k).wait_send()
+
+    for k in range(turn, len(partial_pieces)):
+        send_partial(1, k).wait_send()
+    for k in range(len(partial_pieces)):
+        send_partial(0, k).wait_send()
+    for kind in range(2):
+        for k in range(vector_pieces):
+            send_vectors(kind, k).wait_send()
 
 
 def per_device(rows_n, cols_n, vectors, ham_blocks, ham_columns, bounds):
@@ -194,8 +252,12 @@
     side = REACH * block
     chunks = CHUNKS
     width = vec_width // chunks
+    pieces = []
+    for share in PIECES:
+        start = sum(size for _, size in pieces)
+        pieces.append((start, vec_width * share // sum(PIECES)))
     return pl.pallas_call(
-        functools.partial(kernel, rows_n, cols_n, chunks),
+        functools.partial(kernel, rows_n, cols_n, chunks, VECTOR_PIECES, tuple(pieces)),
         out_shape=jax.ShapeDtypeStruct((height, vec_width), BF16),
         in_specs=[
             pl.BlockSpec(memory_space=pltpu.HBM),
@@ -211,18 +273,22 @@
             pltpu.VMEM((height, height + 2 * side), BF16),
             pltpu.VMEM((2, side, side), BF16),
             pltpu.VMEM((chunks, height, width), BF16),
-            pltpu.VMEM((4, chunks, side, width), BF16),
-            pltpu.VMEM((2, chunks, side, width), BF16),
+            pltpu.VMEM((2, side, vec_width), BF16),
+            pltpu.VMEM((2, side, vec_width), BF16),
+            pltpu.VMEM((2, side, vec_width), BF16),
             pltpu.VMEM((2, chunks, side, width), F32),
-            pltpu.VMEM((2, chunks, side, width), F32),
+            pltpu.VMEM((2, side, vec_width), F32),
             pltpu.VMEM((chunks, height, width), BF16),
-            pltpu.VMEM((2, chunks, side, width), F32),
+            pltpu.VMEM((2, side, vec_width), F32),
             pltpu.SemaphoreType.DMA((chunks,)),
             pltpu.SemaphoreType.DMA,
             pltpu.SemaphoreType.DMA((2,)),
             pltpu.SemaphoreType.REGULAR,
-            pltpu.SemaphoreType.DMA((4, chunks)),
-            pltpu.SemaphoreType.DMA((4, chunks)),
+            pltpu.SemaphoreType.REGULAR,
+            pltpu.SemaphoreType.DMA((2, VECTOR_PIECES)),
+            pltpu.SemaphoreType.DMA((2, VECTOR_PIECES)),
+            pltpu.SemaphoreType.DMA((2, len(pieces))),
+            pltpu.SemaphoreType.DMA((2, len(pieces))),
         ],
         compiler_params=pltpu.CompilerParams(
             collective_id=0, has_side_effects=True, vmem_limit_bytes=VMEM_BYTES

time: 37.5 us -> 36.7 us (0.979)
  the two profiles are of different devices: /device:TPU:1 before, /device:TPU:29 now
where the time goes in v5:
time: 36.7 us; the launch traced here: 36.5 us
  Pallas kernels  35.4 us (96%)
  local copies, waits for them, and re-layouts  1.15 us (3%)
    pallas_call x1, Pallas kernels, per_device(): pl.pallas_call(functools.partial(kernel, rows_n, cols_n, chunks, VECTOR_P...  35.4 us
    unnamed x1, local copies, waits for them, and re-layouts  1.15 us

profile of v5, /device:TPU:29, one launch (start us, length us, event | category | flops | bytes accessed | tf_op | source)
XLA Modules:
  0.0 36.5 jit_solution(1089985104217366076)
XLA Ops:
  0.0 35.4 %shard_map.46 = bf16[768,1024]{1,0:T(8,128)(2,1)S(1)} custom-call(f32[2]{0:T(128)} %bounds_hbm.1, s32[6,5]{1,0:T(8,128)} %columns_hbm.1, bf16[768,1024]{1,0:T(8,128)(2,1)} %vec_hbm.1, bf16[6,5,128,128]{3,2,1,0:T(8,128)(2,1)} %ham_hbm.1), custom_call_target="tpu_custom_call" | custom-call | tf_op jit(solution)/shard_map/pallas_call | solution.py:259
  35.4 1.1 %copy.6 = bf16[768,1024]{1,0:T(8,128)(2,1)} copy(bf16[768,1024]{1,0:T(8,128)(2,1)S(1)} %shard_map.46) | data formatting | bytes 3145728

commit v6 on v5

--- a/solution.py
+++ b/solution.py
@@ -13,7 +13,7 @@
 BF16 = jnp.bfloat16
 CHUNKS = 4
 VECTOR_PIECES = 1
-PIECES = (1, 1, 1, 1)
+PIECES = (4, 3, 1)
 VMEM_BYTES = 20 << 20
 
 
@@ -53,7 +53,7 @@
     follows = at_end - leads
     partner = (row + 1 - 2 * core, col)
 
-    turn = len(partial_pieces) // 2
+    turn = 1
 
     barrier = pltpu.get_barrier_semaphore()
     pl.semaphore_signal(barrier, inc=1, device_id=left, device_id_type=MESH)

time: 36.7 us -> 36.6 us (level)
  no operation moved by 1% of the time
where the time goes in v6:
time: 36.6 us; the launch traced here: 36.5 us
  Pallas kernels  35.3 us (96%)
  local copies, waits for them, and re-layouts  1.15 us (3%)
    pallas_call x1, Pallas kernels, per_device(): pl.pallas_call(functools.partial(kernel, rows_n, cols_n, chunks, VECTOR_P...  35.3 us
    unnamed x1, local copies, waits for them, and re-layouts  1.15 us

profile of v6, /device:TPU:29, one launch (start us, length us, event | category | flops | bytes accessed | tf_op | source)
XLA Modules:
  0.0 36.5 jit_solution(15903503459334740067)
XLA Ops:
  0.0 35.3 %shard_map.46 = bf16[768,1024]{1,0:T(8,128)(2,1)S(1)} custom-call(f32[2]{0:T(128)} %bounds_hbm.1, s32[6,5]{1,0:T(8,128)} %columns_hbm.1, bf16[768,1024]{1,0:T(8,128)(2,1)} %vec_hbm.1, bf16[6,5,128,128]{3,2,1,0:T(8,128)(2,1)} %ham_hbm.1), custom_call_target="tpu_custom_call" | custom-call | tf_op jit(solution)/shard_map/pallas_call | solution.py:259
  35.4 1.1 %copy.6 = bf16[768,1024]{1,0:T(8,128)(2,1)} copy(bf16[768,1024]{1,0:T(8,128)(2,1)S(1)} %shard_map.46) | data formatting | bytes 3145728
